TPU v7x, 32 devices: a whole 2x2x4 slice. The times are simulated.
32 devices in a mesh: row: 8 (over z, x), col: 4 (over y, core).
Axes of the slice: x: 2, y: 2, z: 4, core: 2. Of those that a mesh axis runs over, the one named last changes fastest.
Arguments:
- src_points: bfloat16 [64, 8192], P(None, ('row', 'col')), may hold values from -24 to 24
- tgt_points: bfloat16 [64, 4096], P(None, ('col', 'row')), may hold values from -24 to 24
- grad_f: float32 [8192], P('row'), may hold values from -6 to 6
- grad_g: float32 [4096], P('col'), may hold values from -6 to 6
Outputs:
- grad_src: float32 [64, 8192], P(None, ('row', 'col'))
- grad_tgt: float32 [64, 4096], P(None, ('col', 'row'))
All inputs are finite; a program needn't handle non-finite values.
Results may differ from a plain program's by a relative error of at most 0.0085.
Values may be sent and summed in bfloat16 or wider, within the bound.
No kernel may reach another device: no remote copies, remote signals or barrier semaphores. Data moves between devices by JAX's collectives and lax.ppermute only.
A program may use at most 64 MiB of HBM per device.

v0:
```python
import math
import jax
import jax.numpy as jnp
from jax import lax
from jax.sharding import PartitionSpec as P

SINK = 2
CG = 3
EPS = 4.0
TAU = 0.1


def cost_tile(block_pts, block_sq, points_col, sq_col):
    cross = lax.dot_general(
        block_pts, points_col, (((0,), (0,)), ((), ())), preferred_element_type=jnp.float32
    )
    return block_sq[:, None] + sq_col[None, :] - 2.0 * cross


def body(src_points, tgt_points, grad_f, grad_g):
    points_row = lax.all_gather(src_points, "col", axis=1, tiled=True)
    points_col = lax.all_gather(tgt_points, "row", axis=1, tiled=True)
    sq_row = jnp.sum(jnp.square(points_row.astype(jnp.float32)), axis=0)
    sq_col = jnp.sum(jnp.square(points_col.astype(jnp.float32)), axis=0)
    features, row_count = points_row.shape
    col_count = points_col.shape[1]
    block = min(512, row_count)
    block_count = row_count // block
    blocks_pts = jnp.moveaxis(points_row.reshape(features, block_count, block), 1, 0)
    blocks_sq = sq_row.reshape(block_count, block)
    shift = EPS * math.log(lax.axis_size("row") / lax.axis_size("col"))
    pot_col = jnp.zeros((col_count,), jnp.float32)
    pot_row = jnp.zeros((row_count,), jnp.float32)
    for iteration in range(SINK):

        def row_scores(block_pts, block_sq):
            return (pot_col[None, :] - cost_tile(block_pts, block_sq, points_col, sq_col)) / EPS

        def maxima(pieces):
            return jnp.max(row_scores(pieces[0], pieces[1]), axis=1)

        row_highest = lax.pmax(lax.map(maxima, (blocks_pts, blocks_sq)).reshape(-1), "col")

        def sums(pieces):
            return jnp.sum(jnp.exp(row_scores(pieces[0], pieces[1]) - pieces[2][:, None]), axis=1)

        local = lax.map(
            sums, (blocks_pts, blocks_sq, row_highest.reshape(block_count, block))
        ).reshape(-1)
        row_totals = lax.psum(local, "col")
        pot_row = -EPS * (row_highest + jnp.log(row_totals))
        blocks_pot = pot_row.reshape(block_count, block)

        def scores(pieces):
            return (pieces[2][:, None] - cost_tile(pieces[0], pieces[1], points_col, sq_col)) / EPS

        lowest = jnp.full((col_count,), -jnp.inf, jnp.float32)
        empty = jnp.zeros((col_count,), jnp.float32)

        def max_step(carry, pieces):
            return (jnp.maximum(carry, jnp.max(scores(pieces), axis=0)), None)

        highest, unused = lax.scan(max_step, lowest, (blocks_pts, blocks_sq, blocks_pot))
        highest = lax.pmax(highest, "row")

        def sum_step(carry, pieces):
            return (carry + jnp.sum(jnp.exp(scores(pieces) - highest[None, :]), axis=0), None)

        totals, unused = lax.scan(sum_step, empty, (blocks_pts, blocks_sq, blocks_pot))
        totals = lax.psum(totals, "row")
        pot_col = shift - EPS * (highest + jnp.log(totals))

    def plan_rows(pieces):
        cost = cost_tile(pieces[0], pieces[1], points_col, sq_col)
        return jnp.exp((pieces[2][:, None] + pot_col[None, :] - cost) / EPS).astype(jnp.bfloat16)

    plan_tile = lax.map(
        plan_rows, (blocks_pts, blocks_sq, pot_row.reshape(block_count, block))
    ).reshape(row_count, col_count)

    def row_dot(vector):
        return jnp.sum(plan_tile * vector[None, :], axis=1)

    def col_dot(vector):
        return jnp.sum(plan_tile * vector[:, None], axis=0)

    row_mass = lax.psum(jnp.sum(plan_tile, axis=1, dtype=jnp.float32), "col")
    col_mass, pulled = lax.psum(
        (jnp.sum(plan_tile, axis=0, dtype=jnp.float32), col_dot(grad_f / row_mass)), "row"
    )
    rhs = grad_g - pulled

    def norm_sum(vector):
        return lax.psum(jnp.sum(vector * vector), "col")

    dual_col = jnp.zeros_like(rhs)
    residual = rhs
    direction = rhs
    norm_now = norm_sum(residual)
    for iteration in range(CG):
        applied = lax.psum(row_dot(direction), "col")
        back = lax.psum(col_dot(applied / row_mass), "row")
        image = (1.0 + TAU) * col_mass * direction - back
        alpha = norm_now / lax.psum(jnp.sum(direction * image), "col")
        dual_col = dual_col + alpha * direction
        residual = residual - alpha * image
        norm_next = norm_sum(residual)
        direction = residual + norm_next / norm_now * direction
        norm_now = norm_next
    dual_row = (grad_f - lax.psum(row_dot(dual_col), "col")) / row_mass
    weights = (plan_tile * (dual_row[:, None] + dual_col[None, :])).astype(jnp.bfloat16)
    rows_w = jnp.sum(weights, axis=1, dtype=jnp.float32)
    cols_w = jnp.sum(weights, axis=0, dtype=jnp.float32)
    pulled_src = lax.dot_general(
        points_col, weights, (((1,), (1,)), ((), ())), preferred_element_type=jnp.float32
    )
    pulled_tgt = lax.dot_general(
        points_row, weights, (((1,), (0,)), ((), ())), preferred_element_type=jnp.float32
    )
    part_src = 2.0 * (points_row.astype(jnp.float32) * rows_w[None, :] - pulled_src)
    part_tgt = 2.0 * (points_col.astype(jnp.float32) * cols_w[None, :] - pulled_tgt)
    grad_src = lax.psum_scatter(part_src, "col", scatter_dimension=1, tiled=True)
    grad_tgt = lax.psum_scatter(part_tgt, "row", scatter_dimension=1, tiled=True)
    return (grad_src, grad_tgt)


def solution(mesh):
    in_specs = (P(None, ("row", "col")), P(None, ("col", "row")), P("row"), P("col"))
    out_specs = (P(None, ("row", "col")), P(None, ("col", "row")))
    return jax.shard_map(body, mesh=mesh, in_specs=in_specs, out_specs=out_specs, check_vma=False)
```

profile of v0, /device:TPU:0, one launch (start us, length us, event | category | flops | bytes accessed | tf_op | source)
XLA Modules:
  0.0 396.4 jit_solution(7634466997313843352)
XLA Ops:
  7.3 28.2 %all_gather.7 = bf16[64,1024]{1,0:T(8,128)(2,1)S(1)} all-gather(bf16[64,128]{1,0:T(8,128)(2,1)} %param.23), channel_id=1, replica_groups=mesh['row'=8,'col'=4] {'row'}, dimensions={1}, use_global_device_ids=true | all-gather | bytes 147456 | tf_op jit(solution)/shard_map/all_gather | solution.py:22
  35.4 5.6 %all_gather.6 = bf16[64,1024]{1,0:T(8,128)(2,1)S(1)} all-gather(bf16[64,256]{1,0:T(8,128)(2,1)} %param.22), channel_id=1, replica_groups=mesh['row'=8,'col'=4] {'col'}, dimensions={1}, use_global_device_ids=true | all-gather | bytes 163840 | tf_op jit(solution)/shard_map/all_gather | solution.py:21
  41.2 1.5 while.94
  41.2 0.7 multiply_reduce_fusion.14
  41.9 0.7 multiply_reduce_fusion.14
  42.7 7.1 %pmax.28 = f32[1024]{0:T(1024)S(1)} all-reduce(f32[1024]{0:T(1024)S(1)} %bitcast.218), channel_id=1, replica_groups=mesh['row'=8,'col'=4] {'col'}, use_global_device_ids=true, to_apply=%region_5.6 | all-reduce | flops 1024 | bytes 8192 | tf_op jit(solution)/shard_map/pmax | solution.py:42
  49.8 1.9 while.95
  49.9 0.9 exponential_reduce_fusion.8
  50.8 0.9 exponential_reduce_fusion.8
  51.8 5.9 %psum.140 = f32[1024]{0:T(1024)S(1)} all-reduce(f32[1024]{0:T(1024)S(1)} %bitcast.219), channel_id=1, replica_groups=mesh['row'=8,'col'=4] {'col'}, use_global_device_ids=true, to_apply=%region_9.10 | all-reduce | flops 1024 | bytes 8192 | tf_op jit(solution)/shard_map/psum | solution.py:50
  57.7 1.3 while.99
  57.7 0.6 multiply_reduce_fusion.16
  58.4 0.6 multiply_reduce_fusion.16
  59.1 19.7 %pmax.29 = f32[1024]{0:T(1024)S(1)} all-reduce(f32[1024]{0:T(1024)S(1)} %get-tuple-element.352), channel_id=1, replica_groups=mesh['row'=8,'col'=4] {'row'}, use_global_device_ids=true, to_apply=%region_13.14 | all-reduce | flops 1024 | bytes 8192 | tf_op jit(solution)/shard_map/pmax | solution.py:64
  78.8 1.8 while.100
  78.8 0.8 exponential_reduce_fusion.10
  79.7 0.8 exponential_reduce_fusion.10
  80.5 17.1 %psum.141 = f32[1024]{0:T(1024)S(1)} all-reduce(f32[1024]{0:T(1024)S(1)} %get-tuple-element.353), channel_id=1, replica_groups=mesh['row'=8,'col'=4] {'row'}, use_global_device_ids=true, to_apply=%region_17.18 | all-reduce | flops 1024 | bytes 8192 | tf_op jit(solution)/shard_map/psum | solution.py:70
  97.7 1.5 while.96
  97.7 0.7 multiply_reduce_fusion.15
  98.5 0.7 multiply_reduce_fusion.15
  99.2 5.8 %pmax.30 = f32[1024]{0:T(1024)S(1)} all-reduce(f32[1024]{0:T(1024)S(1)} %bitcast.220), channel_id=1, replica_groups=mesh['row'=8,'col'=4] {'col'}, use_global_device_ids=true, to_apply=%region_21.22 | all-reduce | flops 1024 | bytes 8192 | tf_op jit(solution)/shard_map/pmax | solution.py:42
  105.0 1.9 while.97
  105.0 0.9 exponential_reduce_fusion.9
  106.0 0.9 exponential_reduce_fusion.9
  107.0 5.8 %psum.142 = f32[1024]{0:T(1024)S(1)} all-reduce(f32[1024]{0:T(1024)S(1)} %bitcast.221), channel_id=1, replica_groups=mesh['row'=8,'col'=4] {'col'}, use_global_device_ids=true, to_apply=%region_25.26 | all-reduce | flops 1024 | bytes 8192 | tf_op jit(solution)/shard_map/psum | solution.py:50
  112.8 1.3 while.101
  112.8 0.6 multiply_reduce_fusion.17
  113.5 0.6 multiply_reduce_fusion.17
  114.1 19.1 %pmax.31 = f32[1024]{0:T(1024)S(1)} all-reduce(f32[1024]{0:T(1024)S(1)} %get-tuple-element.356), channel_id=1, replica_groups=mesh['row'=8,'col'=4] {'row'}, use_global_device_ids=true, to_apply=%region_29.30 | all-reduce | flops 1024 | bytes 8192 | tf_op jit(solution)/shard_map/pmax | solution.py:64
  133.2 1.8 while.102
  133.3 0.8 exponential_reduce_fusion.11
  134.1 0.8 exponential_reduce_fusion.11
  135.0 17.1 %psum.143 = f32[1024]{0:T(1024)S(1)} all-reduce(f32[1024]{0:T(1024)S(1)} %get-tuple-element.357), channel_id=1, replica_groups=mesh['row'=8,'col'=4] {'row'}, use_global_device_ids=true, to_apply=%region_33.34 | all-reduce | flops 1024 | bytes 8192 | tf_op jit(solution)/shard_map/psum | solution.py:70
  152.2 1.7 while.98
  152.2 0.8 fusion.87
  153.0 0.8 fusion.87
  153.9 0.9 convert_reduce_fusion
  154.8 5.7 %psum.144 = f32[1024]{0:T(1024)S(1)} all-reduce(f32[1024]{0:T(1024)S(1)} %bitcast.222), channel_id=1, replica_groups=mesh['row'=8,'col'=4] {'col'}, use_global_device_ids=true, to_apply=%region_37.38 | all-reduce | flops 1024 | bytes 8192 | tf_op jit(solution)/shard_map/psum | solution.py:87
  161.0 19.1 %psum.145 = f32[1024]{0:T(1024)S(1)} all-reduce(f32[1024]{0:T(1024)S(1)} %fusion.29), channel_id=1, replica_groups=mesh['row'=8,'col'=4] {'row'}, use_global_device_ids=true, to_apply=%region_39.40 | all-reduce | flops 1024 | bytes 8192 | tf_op jit(solution)/shard_map/psum | solution.py:88
  180.6 5.7 %psum.148 = f32[1024]{0:T(1024)S(1)} all-reduce(f32[1024]{0:T(1024)S(1)} %bitcast.223), channel_id=1, replica_groups=mesh['row'=8,'col'=4] {'col'}, use_global_device_ids=true, to_apply=%region_45.46 | all-reduce | flops 1024 | bytes 8192 | tf_op jit(solution)/shard_map/psum | solution.py:101
  186.8 17.4 %all-reduce = (f32[1024]{0:T(1024)S(1)}, f32[1024]{0:T(1024)S(1)}) all-reduce(f32[1024]{0:T(1024)S(1)} %fusion.31, f32[1024]{0:T(1024)S(1)} %get-tuple-element.463), channel_id=1, replica_groups=mesh['row'=8,'col'=4] {'row'}, use_global_device_ids=true, to_apply=%region_47.48 | all-reduce | flops 2048 | bytes 16384 | tf_op jit(solution)/shard_map/psum | solution.py:102
  204.2 0.6 multiply_reduce_fusion.8
  204.8 6.3 %all-reduce.1 = (f32[]{:T(128)}, f32[]{:T(128)}) all-reduce(f32[]{:T(128)} %get-tuple-element.466, f32[]{:T(128)} %get-tuple-element.465), channel_id=1, replica_groups=mesh['row'=8,'col'=4] {'col'}, use_global_device_ids=true, to_apply=%region_41.42 | all-reduce | flops 2 | bytes 16 | tf_op jit(solution)/shard_map/psum | solution.py:94
  212.4 0.6 multiply_reduce_fusion.7
  213.0 7.5 %psum.151 = f32[]{:T(128)} all-reduce(f32[]{:T(128)} %get-tuple-element.605), channel_id=1, replica_groups=mesh['row'=8,'col'=4] {'col'}, use_global_device_ids=true, to_apply=%region_51.52 | all-reduce | flops 1 | bytes 8 | tf_op jit(solution)/shard_map/psum | solution.py:94
  221.9 0.5 fusion.32
  222.4 5.7 %psum.152 = f32[1024]{0:T(1024)S(1)} all-reduce(f32[1024]{0:T(1024)S(1)} %bitcast.224), channel_id=1, replica_groups=mesh['row'=8,'col'=4] {'col'}, use_global_device_ids=true, to_apply=%region_53.54 | all-reduce | flops 1024 | bytes 8192 | tf_op jit(solution)/shard_map/psum | solution.py:101
  228.5 19.2 %psum.153 = f32[1024]{0:T(1024)S(1)} all-reduce(f32[1024]{0:T(1024)S(1)} %fusion.33), channel_id=1, replica_groups=mesh['row'=8,'col'=4] {'row'}, use_global_device_ids=true, to_apply=%region_55.56 | all-reduce | flops 1024 | bytes 8192 | tf_op jit(solution)/shard_map/psum | solution.py:102
  247.7 0.6 multiply_reduce_fusion.6
  248.3 6.3 %psum.154 = f32[]{:T(128)} all-reduce(f32[]{:T(128)} %multiply_reduce_fusion.6), channel_id=1, replica_groups=mesh['row'=8,'col'=4] {'col'}, use_global_device_ids=true, to_apply=%region_57.58 | all-reduce | flops 1 | bytes 8 | tf_op jit(solution)/shard_map/psum | solution.py:104
  255.9 0.6 multiply_reduce_fusion.5
  256.5 6.7 %psum.155 = f32[]{:T(128)} all-reduce(f32[]{:T(128)} %get-tuple-element.603), channel_id=1, replica_groups=mesh['row'=8,'col'=4] {'col'}, use_global_device_ids=true, to_apply=%region_59.60 | all-reduce | flops 1 | bytes 8 | tf_op jit(solution)/shard_map/psum | solution.py:94
  265.0 5.7 %psum.156 = f32[1024]{0:T(1024)S(1)} all-reduce(f32[1024]{0:T(1024)S(1)} %bitcast.225), channel_id=1, replica_groups=mesh['row'=8,'col'=4] {'col'}, use_global_device_ids=true, to_apply=%region_61.62 | all-reduce | flops 1024 | bytes 8192 | tf_op jit(solution)/shard_map/psum | solution.py:101
  271.2 17.1 %psum.157 = f32[1024]{0:T(1024)S(1)} all-reduce(f32[1024]{0:T(1024)S(1)} %fusion.35), channel_id=1, replica_groups=mesh['row'=8,'col'=4] {'row'}, use_global_device_ids=true, to_apply=%region_63.64 | all-reduce | flops 1024 | bytes 8192 | tf_op jit(solution)/shard_map/psum | solution.py:102
  288.4 0.6 multiply_reduce_fusion.4
  289.0 6.3 %psum.158 = f32[]{:T(128)} all-reduce(f32[]{:T(128)} %multiply_reduce_fusion.4), channel_id=1, replica_groups=mesh['row'=8,'col'=4] {'col'}, use_global_device_ids=true, to_apply=%region_65.66 | all-reduce | flops 1 | bytes 8 | tf_op jit(solution)/shard_map/psum | solution.py:104
  297.1 6.7 %psum.159 = f32[1024]{0:T(1024)S(1)} all-reduce(f32[1024]{0:T(1024)S(1)} %bitcast.226), channel_id=1, replica_groups=mesh['row'=8,'col'=4] {'col'}, use_global_device_ids=true, to_apply=%region_67.68 | all-reduce | flops 1024 | bytes 8192 | tf_op jit(solution)/shard_map/psum | solution.py:110
  303.8 0.5 fusion.38
  304.4 1.0 convert_reduce_fusion.2
  305.7 1.2 fusion.40
  307.0 3.1 fusion.42
  310.1 57.3 %reduce-scatter.5.cloned.1.call-done = f32[64,128]{1,0:T(8,128)} async-done(((f32[64,1024]{1,0:T(8,128)}), f32[64,128]{1,0:T(8,128)}) %reduce-scatter.5.cloned.1.call-update) | async-done | bytes 32784 | tf_op jit(solution)/shard_map/reduce_scatter | solution.py:123
  367.5 22.1 %reduce-scatter.3.cloned.1.call-done = f32[64,256]{1,0:T(8,128)} async-done(((f32[64,1024]{1,0:T(8,128)}), f32[64,256]{1,0:T(8,128)}) %reduce-scatter.3.cloned.1.call-update) | async-done | bytes 65552 | tf_op jit(solution)/shard_map/reduce_scatter | solution.py:122
  (96 shorter events, 4.8 us)
Async XLA Ops:
  7.2 360.3 %reduce-scatter.5.cloned.1.call-start = ((), (), s32[]{:S(2)}) async-start(), calls=%async_computation.3 | async-start | bytes 294912 | tf_op jit(solution)/shard_map/reduce_scatter | solution.py:123
  153.9 6.6 %copy-start.1 = (f32[1024]{0:T(1024)S(1)}, f32[1024]{0:T(1024)}, u32[]{:S(2)}) copy-start(f32[1024]{0:T(1024)} %param.24) | copy-start | bytes 12292
  153.9 26.2 %copy-start.2 = (f32[1024]{0:T(1024)S(1)}, f32[1024]{0:T(1024)}, u32[]{:S(2)}) copy-start(f32[1024]{0:T(1024)} %param.25) | copy-start | bytes 12292
  304.4 1.4 copy-start
  306.9 82.7 %reduce-scatter.3.cloned.1.call-start = ((), (), s32[]{:S(2)}) async-start(), calls=%async_computation.2 | async-start | bytes 327680 | tf_op jit(solution)/shard_map/reduce_scatter | solution.py:122
Sparse Core Ops, SparseCore 0:
  307.1 60.3 reduce-scatter.4
  370.5 19.0 reduce-scatter.2
where the time goes:
time: 397 us; the launch traced here: 396 us
  blocking collectives  267 us (67%)
  waiting for transfers between devices  79.5 us (20%)
  between operations  21 us (5%)
  matrix products  18.1 us (5%)
  other arithmetic  9.57 us (2%)
    reduce_scatter x1, waiting for transfers between devices, body(): lax.psum_scatter(part_tgt, 'row', scatter_dimension=1, tiled=True)  57.3 us
    psum x3, blocking collectives, body(): back = lax.psum(col_dot(applied / row_mass), 'row')  53.7 us
    pmax x2, blocking collectives, body(): highest = lax.pmax(highest, 'row')  38.8 us
    psum x2, blocking collectives, body(): totals = lax.psum(totals, 'row')  34.3 us
    all_gather x1, blocking collectives, body(): points_col = lax.all_gather(tgt_points, 'row', axis=1, tiled=True)  28.2 us
    reduce_scatter x1, waiting for transfers between devices, body(): lax.psum_scatter(part_src, 'col', scatter_dimension=1, tiled=True)  22.1 us
    psum x3, blocking collectives, norm_sum(): return lax.psum(jnp.sum(vector * vector), 'col')  20.4 us
    psum x1, blocking collectives, body(): lax.psum((jnp.sum(plan_tile, axis=0, dtype=jnp.float32), col_dot(grad_f /...  19.1 us
  transfers between devices with their start and end apart: 2, of which 2 were waited for; matrix products, arithmetic and copies ran while one was open for 1% of the time, Pallas kernels for 0%

commit v1 on v0

--- a/solution.py
+++ b/solution.py
@@ -99,7 +99,7 @@
     norm_now = norm_sum(residual)
     for iteration in range(CG):
         applied = lax.psum(row_dot(direction), "col")
-        back = lax.psum(col_dot(applied / row_mass), "row")
+        back = jnp.sum(lax.all_gather(col_dot(applied / row_mass), "row"), axis=0)
         image = (1.0 + TAU) * col_mass * direction - back
         alpha = norm_now / lax.psum(jnp.sum(direction * image), "col")
         dual_col = dual_col + alpha * direction

time: 397 us -> 434 us (1.093)
  blocking collectives: 267 us -> 305 us
    all_gather x0 -> x3, blocking collectives: none -> 91.8 us  [body(): back = jnp.sum(lax.all_gather(col_dot(applied / row_mass), 'row'), axis=0)]
    psum x3 -> x0, blocking collectives: 53.7 us -> none  [body(): back = lax.psum(col_dot(applied / row_mass), 'row')]
where the time goes in v1:
time: 434 us; the launch traced here: 433 us
  blocking collectives  305 us (70%)
  waiting for transfers between devices  78.1 us (18%)
  between operations  21.1 us (5%)
  matrix products  18.1 us (4%)
  other arithmetic  9.61 us (2%)
    all_gather x3, blocking collectives, body(): back = jnp.sum(lax.all_gather(col_dot(applied / row_mass), 'row'), axis=0)  91.8 us
    reduce_scatter x1, waiting for transfers between devices, body(): lax.psum_scatter(part_tgt, 'row', scatter_dimension=1, tiled=True)  55.8 us
    pmax x2, blocking collectives, body(): highest = lax.pmax(highest, 'row')  38.8 us
    psum x2, blocking collectives, body(): totals = lax.psum(totals, 'row')  34.3 us
    all_gather x1, blocking collectives, body(): points_col = lax.all_gather(tgt_points, 'row', axis=1, tiled=True)  28.2 us
    reduce_scatter x1, waiting for transfers between devices, body(): lax.psum_scatter(part_src, 'col', scatter_dimension=1, tiled=True)  22.2 us
    psum x3, blocking collectives, norm_sum(): return lax.psum(jnp.sum(vector * vector), 'col')  20.4 us
    psum x1, blocking collectives, body(): lax.psum((jnp.sum(plan_tile, axis=0, dtype=jnp.float32), col_dot(grad_f /...  19.4 us
  transfers between devices with their start and end apart: 2, of which 2 were waited for; matrix products, arithmetic and copies ran while one was open for 1% of the time, Pallas kernels for 0%

profile of v1, /device:TPU:0, one launch (start us, length us, event | category | flops | bytes accessed | tf_op | source)
XLA Modules:
  0.0 433.5 jit_solution(11187604535859390233)
XLA Ops:
  7.3 28.2 %all_gather.25 = bf16[64,1024]{1,0:T(8,128)(2,1)S(1)} all-gather(bf16[64,128]{1,0:T(8,128)(2,1)} %param.23), channel_id=1, replica_groups=mesh['row'=8,'col'=4] {'row'}, dimensions={1}, use_global_device_ids=true | all-gather | bytes 147456 | tf_op jit(solution)/shard_map/all_gather | solution.py:22
  35.4 5.6 %all_gather.24 = bf16[64,1024]{1,0:T(8,128)(2,1)S(1)} all-gather(bf16[64,256]{1,0:T(8,128)(2,1)} %param.22), channel_id=1, replica_groups=mesh['row'=8,'col'=4] {'col'}, dimensions={1}, use_global_device_ids=true | all-gather | bytes 163840 | tf_op jit(solution)/shard_map/all_gather | solution.py:21
  41.2 1.5 while.94
  41.2 0.7 multiply_reduce_fusion.14
  41.9 0.7 multiply_reduce_fusion.14
  42.7 7.1 %pmax.28 = f32[1024]{0:T(1024)S(1)} all-reduce(f32[1024]{0:T(1024)S(1)} %bitcast.218), channel_id=1, replica_groups=mesh['row'=8,'col'=4] {'col'}, use_global_device_ids=true, to_apply=%region_5.6 | all-reduce | flops 1024 | bytes 8192 | tf_op jit(solution)/shard_map/pmax | solution.py:42
  49.8 1.9 while.95
  49.9 0.9 exponential_reduce_fusion.8
  50.8 0.9 exponential_reduce_fusion.8
  51.8 5.9 %psum.119 = f32[1024]{0:T(1024)S(1)} all-reduce(f32[1024]{0:T(1024)S(1)} %bitcast.219), channel_id=1, replica_groups=mesh['row'=8,'col'=4] {'col'}, use_global_device_ids=true, to_apply=%region_9.10 | all-reduce | flops 1024 | bytes 8192 | tf_op jit(solution)/shard_map/psum | solution.py:50
  57.7 1.3 while.99
  57.7 0.6 multiply_reduce_fusion.16
  58.4 0.6 multiply_reduce_fusion.16
  59.1 19.7 %pmax.29 = f32[1024]{0:T(1024)S(1)} all-reduce(f32[1024]{0:T(1024)S(1)} %get-tuple-element.352), channel_id=1, replica_groups=mesh['row'=8,'col'=4] {'row'}, use_global_device_ids=true, to_apply=%region_13.14 | all-reduce | flops 1024 | bytes 8192 | tf_op jit(solution)/shard_map/pmax | solution.py:64
  78.8 1.8 while.100
  78.8 0.8 exponential_reduce_fusion.10
  79.7 0.8 exponential_reduce_fusion.10
  80.5 17.1 %psum.120 = f32[1024]{0:T(1024)S(1)} all-reduce(f32[1024]{0:T(1024)S(1)} %get-tuple-element.353), channel_id=1, replica_groups=mesh['row'=8,'col'=4] {'row'}, use_global_device_ids=true, to_apply=%region_17.18 | all-reduce | flops 1024 | bytes 8192 | tf_op jit(solution)/shard_map/psum | solution.py:70
  97.7 1.5 while.96
  97.7 0.7 multiply_reduce_fusion.15
  98.5 0.7 multiply_reduce_fusion.15
  99.2 5.8 %pmax.30 = f32[1024]{0:T(1024)S(1)} all-reduce(f32[1024]{0:T(1024)S(1)} %bitcast.220), channel_id=1, replica_groups=mesh['row'=8,'col'=4] {'col'}, use_global_device_ids=true, to_apply=%region_21.22 | all-reduce | flops 1024 | bytes 8192 | tf_op jit(solution)/shard_map/pmax | solution.py:42
  105.0 1.9 while.97
  105.0 0.9 exponential_reduce_fusion.9
  106.0 0.9 exponential_reduce_fusion.9
  107.0 5.8 %psum.121 = f32[1024]{0:T(1024)S(1)} all-reduce(f32[1024]{0:T(1024)S(1)} %bitcast.221), channel_id=1, replica_groups=mesh['row'=8,'col'=4] {'col'}, use_global_device_ids=true, to_apply=%region_25.26 | all-reduce | flops 1024 | bytes 8192 | tf_op jit(solution)/shard_map/psum | solution.py:50
  112.8 1.3 while.101
  112.8 0.6 multiply_reduce_fusion.17
  113.5 0.6 multiply_reduce_fusion.17
  114.1 19.1 %pmax.31 = f32[1024]{0:T(1024)S(1)} all-reduce(f32[1024]{0:T(1024)S(1)} %get-tuple-element.356), channel_id=1, replica_groups=mesh['row'=8,'col'=4] {'row'}, use_global_device_ids=true, to_apply=%region_29.30 | all-reduce | flops 1024 | bytes 8192 | tf_op jit(solution)/shard_map/pmax | solution.py:64
  133.2 1.8 while.102
  133.3 0.8 exponential_reduce_fusion.11
  134.1 0.8 exponential_reduce_fusion.11
  135.0 17.1 %psum.122 = f32[1024]{0:T(1024)S(1)} all-reduce(f32[1024]{0:T(1024)S(1)} %get-tuple-element.357), channel_id=1, replica_groups=mesh['row'=8,'col'=4] {'row'}, use_global_device_ids=true, to_apply=%region_33.34 | all-reduce | flops 1024 | bytes 8192 | tf_op jit(solution)/shard_map/psum | solution.py:70
  152.2 1.7 while.98
  152.2 0.8 fusion.87
  153.0 0.8 fusion.87
  153.9 0.9 convert_reduce_fusion
  154.8 5.7 %psum.123 = f32[1024]{0:T(1024)S(1)} all-reduce(f32[1024]{0:T(1024)S(1)} %bitcast.222), channel_id=1, replica_groups=mesh['row'=8,'col'=4] {'col'}, use_global_device_ids=true, to_apply=%region_37.38 | all-reduce | flops 1024 | bytes 8192 | tf_op jit(solution)/shard_map/psum | solution.py:87
  161.0 19.4 %all-reduce = (f32[1024]{0:T(1024)S(1)}, f32[1024]{0:T(1024)S(1)}) all-reduce(f32[1024]{0:T(1024)S(1)} %fusion.29, f32[1024]{0:T(1024)S(1)} %get-tuple-element.463), channel_id=1, replica_groups=mesh['row'=8,'col'=4] {'row'}, use_global_device_ids=true, to_apply=%region_39.40 | all-reduce | flops 2048 | bytes 16384 | tf_op jit(solution)/shard_map/psum | solution.py:88
  180.9 5.7 %psum.127 = f32[1024]{0:T(1024)S(1)} all-reduce(f32[1024]{0:T(1024)S(1)} %bitcast.223), channel_id=1, replica_groups=mesh['row'=8,'col'=4] {'col'}, use_global_device_ids=true, to_apply=%region_45.46 | all-reduce | flops 1024 | bytes 8192 | tf_op jit(solution)/shard_map/psum | solution.py:101
  187.1 30.6 %all-gather = f32[8192]{0:T(1024)S(1)} all-gather(f32[1024]{0:T(1024)S(1)} %fusion.31), channel_id=2, replica_groups=mesh['row'=8,'col'=4] {'row'}, dimensions={0}, use_global_device_ids=true | all-gather | bytes 36864 | tf_op jit(solution)/shard_map/all_gather | solution.py:102
  217.7 0.6 multiply_reduce_fusion.8
  218.3 6.3 %all-reduce.1 = (f32[]{:T(128)}, f32[]{:T(128)}) all-reduce(f32[]{:T(128)} %get-tuple-element.466, f32[]{:T(128)} %get-tuple-element.465), channel_id=1, replica_groups=mesh['row'=8,'col'=4] {'col'}, use_global_device_ids=true, to_apply=%region_41.42 | all-reduce | flops 2 | bytes 16 | tf_op jit(solution)/shard_map/psum | solution.py:94
  225.9 0.6 multiply_reduce_fusion.7
  226.5 7.5 %psum.129 = f32[]{:T(128)} all-reduce(f32[]{:T(128)} %get-tuple-element.605), channel_id=1, replica_groups=mesh['row'=8,'col'=4] {'col'}, use_global_device_ids=true, to_apply=%region_51.52 | all-reduce | flops 1 | bytes 8 | tf_op jit(solution)/shard_map/psum | solution.py:94
  235.4 0.5 fusion.32
  235.9 5.7 %psum.130 = f32[1024]{0:T(1024)S(1)} all-reduce(f32[1024]{0:T(1024)S(1)} %bitcast.224), channel_id=1, replica_groups=mesh['row'=8,'col'=4] {'col'}, use_global_device_ids=true, to_apply=%region_53.54 | all-reduce | flops 1024 | bytes 8192 | tf_op jit(solution)/shard_map/psum | solution.py:101
  242.0 30.6 %all-gather.1 = f32[8192]{0:T(1024)S(1)} all-gather(f32[1024]{0:T(1024)S(1)} %fusion.33), channel_id=3, replica_groups=mesh['row'=8,'col'=4] {'row'}, dimensions={0}, use_global_device_ids=true | all-gather | bytes 36864 | tf_op jit(solution)/shard_map/all_gather | solution.py:102
  272.7 0.6 multiply_reduce_fusion.6
  273.3 6.3 %psum.131 = f32[]{:T(128)} all-reduce(f32[]{:T(128)} %multiply_reduce_fusion.6), channel_id=1, replica_groups=mesh['row'=8,'col'=4] {'col'}, use_global_device_ids=true, to_apply=%region_57.58 | all-reduce | flops 1 | bytes 8 | tf_op jit(solution)/shard_map/psum | solution.py:104
  280.9 0.6 multiply_reduce_fusion.5
  281.5 6.7 %psum.132 = f32[]{:T(128)} all-reduce(f32[]{:T(128)} %get-tuple-element.603), channel_id=1, replica_groups=mesh['row'=8,'col'=4] {'col'}, use_global_device_ids=true, to_apply=%region_59.60 | all-reduce | flops 1 | bytes 8 | tf_op jit(solution)/shard_map/psum | solution.py:94
  290.0 5.7 %psum.133 = f32[1024]{0:T(1024)S(1)} all-reduce(f32[1024]{0:T(1024)S(1)} %bitcast.225), channel_id=1, replica_groups=mesh['row'=8,'col'=4] {'col'}, use_global_device_ids=true, to_apply=%region_61.62 | all-reduce | flops 1024 | bytes 8192 | tf_op jit(solution)/shard_map/psum | solution.py:101
  296.2 30.6 %all-gather.2 = f32[8192]{0:T(1024)S(1)} all-gather(f32[1024]{0:T(1024)S(1)} %fusion.35), channel_id=4, replica_groups=mesh['row'=8,'col'=4] {'row'}, dimensions={0}, use_global_device_ids=true | all-gather | bytes 36864 | tf_op jit(solution)/shard_map/all_gather | solution.py:102
  326.9 0.6 multiply_reduce_fusion.4
  327.5 6.3 %psum.134 = f32[]{:T(128)} all-reduce(f32[]{:T(128)} %multiply_reduce_fusion.4), channel_id=1, replica_groups=mesh['row'=8,'col'=4] {'col'}, use_global_device_ids=true, to_apply=%region_65.66 | all-reduce | flops 1 | bytes 8 | tf_op jit(solution)/shard_map/psum | solution.py:104
  335.6 6.7 %psum.135 = f32[1024]{0:T(1024)S(1)} all-reduce(f32[1024]{0:T(1024)S(1)} %bitcast.226), channel_id=1, replica_groups=mesh['row'=8,'col'=4] {'col'}, use_global_device_ids=true, to_apply=%region_67.68 | all-reduce | flops 1024 | bytes 8192 | tf_op jit(solution)/shard_map/psum | solution.py:110
  342.3 0.6 fusion.38
  342.9 1.0 convert_reduce_fusion.2
  344.2 1.2 fusion.40
  345.5 3.1 fusion.42
  348.6 55.8 %reduce-scatter.5.cloned.1.call-done = f32[64,128]{1,0:T(8,128)} async-done(((f32[64,1024]{1,0:T(8,128)}), f32[64,128]{1,0:T(8,128)}) %reduce-scatter.5.cloned.1.call-update) | async-done | bytes 32784 | tf_op jit(solution)/shard_map/reduce_scatter | solution.py:123
  404.4 22.2 %reduce-scatter.3.cloned.1.call-done = f32[64,256]{1,0:T(8,128)} async-done(((f32[64,1024]{1,0:T(8,128)}), f32[64,256]{1,0:T(8,128)}) %reduce-scatter.3.cloned.1.call-update) | async-done | bytes 65552 | tf_op jit(solution)/shard_map/reduce_scatter | solution.py:122
  (102 shorter events, 4.9 us)
Async XLA Ops:
  7.2 397.3 %reduce-scatter.5.cloned.1.call-start = ((), (), s32[]{:S(2)}) async-start(), calls=%async_computation.3 | async-start | bytes 294912 | tf_op jit(solution)/shard_map/reduce_scatter | solution.py:123
  153.9 6.6 %copy-start.1 = (f32[1024]{0:T(1024)S(1)}, f32[1024]{0:T(1024)}, u32[]{:S(2)}) copy-start(f32[1024]{0:T(1024)} %param.24) | copy-start | bytes 12292
  153.9 26.5 %copy-start.2 = (f32[1024]{0:T(1024)S(1)}, f32[1024]{0:T(1024)}, u32[]{:S(2)}) copy-start(f32[1024]{0:T(1024)} %param.25) | copy-start | bytes 12292
  342.9 1.4 copy-start
  345.4 81.2 %reduce-scatter.3.cloned.1.call-start = ((), (), s32[]{:S(2)}) async-start(), calls=%async_computation.2 | async-start | bytes 327680 | tf_op jit(solution)/shard_map/reduce_scatter | solution.py:122
Sparse Core Ops, SparseCore 0:
  345.6 58.8 reduce-scatter.4
  407.5 19.1 reduce-scatter.2
